TPU v7x, 256 devices: a whole 4x4x8 slice. The times are simulated.
256 devices in a mesh: seq: 64 (over z, y, x_hi), tp: 4 (over x_lo, core).
Axes of the slice: x: 4 (x_hi: 2, x_lo: 2; x = x_hi * 2 + x_lo), y: 4, z: 8, core: 2. Of those that a mesh axis runs over, the one named last changes fastest.
Arguments:
- latents: bfloat16 [16384, 5120], P('seq', 'tp'), may hold values from -6 to 6
- noise: bfloat16 [16384, 5120], P('seq', 'tp'), may hold values from -6 to 6
- tstep: int32 [256], P('seq'), may hold values from 0 to 999
- offsets: int32 [256], P('seq'), may hold values from -64 to 64, as said below
- teacher_heads: bfloat16 [16384, 2560], P('seq', 'tp'), may hold values from -6 to 6
- teacher_proj: bfloat16 [2560, 5120], P('tp', 'seq'), may hold values from -0.125 to 0.125
- queries: bfloat16 [16384, 2560], P('seq', 'tp'), may hold values from -200 to 200
- keys: bfloat16 [16384, 2560], P('seq', 'tp'), may hold values from -6 to 6
- values: bfloat16 [16384, 2560], P('seq', 'tp'), may hold values from -6 to 6
- query_tangent: bfloat16 [16384, 2560], P('seq', 'tp'), may hold values from -6 to 6
- key_tangent: bfloat16 [16384, 2560], P('seq', 'tp'), may hold values from -6 to 6
- value_tangent: bfloat16 [16384, 2560], P('seq', 'tp'), may hold values from -6 to 6
- out_proj: bfloat16 [2560, 5120], P('tp', 'seq'), may hold values from -0.125 to 0.125
Outputs:
- student_out: float32 [16384, 5120], P('seq', 'tp')
- student_tangent: float32 [16384, 5120], P('seq', 'tp')
Inputs may be any that keep to these rules, and one draw needn't show every extreme that they name: `offsets`: both ends, -64 and 64, occur in every draw.
All inputs are finite; a program needn't handle non-finite values.
Results may differ from a plain program's by a relative error of at most 0.0045.
Values may be sent and summed in bfloat16 or wider, within the bound.
No kernel may reach another device: no remote copies, remote signals or barrier semaphores. Data moves between devices by JAX's collectives and lax.ppermute only.
A program may use at most 128 MiB of HBM per device.

v0:
```python
import math
import jax
import jax.numpy as jnp
from jax import lax
from jax.sharding import PartitionSpec as P

HD = 128
WIN = 256
OFF = 64
BLK = 64
STEPS = 1000


def padded_2(block, sides, width):
    for axis, dim in sides:
        count = lax.axis_size(axis)
        forward = [(i, i + 1) for i in range(count - 1)]
        backward = [(target, source) for source, target in forward]
        low = lax.ppermute(
            lax.slice_in_dim(block, block.shape[dim] - width, None, axis=dim), axis, forward
        )
        high = lax.ppermute(lax.slice_in_dim(block, 0, width, axis=dim), axis, backward)
        block = jnp.concatenate([low, block, high], axis=dim)
    return block


def body(
    latents,
    noise,
    tstep,
    offsets,
    teacher_heads,
    teacher_proj,
    queries,
    keys,
    values,
    query_tangent,
    key_tangent,
    value_tangent,
    out_proj,
):
    tokens_here = latents.shape[0]
    width_here = queries.shape[1]
    heads_here = width_here // HD
    reach = WIN // 2 + OFF
    score_scale = 1.0 / math.sqrt(HD)
    step_time = (tstep.astype(jnp.float32) + 0.5) * (math.pi / (2 * STEPS))
    per_token = jnp.repeat(step_time, BLK)[:, None]
    cosine = jnp.cos(per_token)
    sine_t = jnp.sin(per_token)
    noisy = cosine * latents.astype(jnp.float32) + sine_t * noise.astype(jnp.float32)
    teacher_term = jnp.dot(
        teacher_heads,
        lax.all_gather(teacher_proj, "seq", axis=1, tiled=True),
        preferred_element_type=jnp.float32,
    )
    velocity = lax.psum_scatter(teacher_term, "tp", scatter_dimension=1, tiled=True)
    stacked = jnp.stack([keys, values, key_tangent, value_tangent], 0)
    padded = padded_2(stacked, (("seq", 1),), reach)
    padded = padded.reshape(4, tokens_here + 2 * reach, heads_here, HD)
    first_pos = lax.axis_index("seq") * tokens_here
    total_tokens = tokens_here * lax.axis_size("seq")
    block_count = tokens_here // BLK
    span = BLK + WIN
    block_low = offsets - WIN // 2
    starts = jnp.arange(block_count, dtype=jnp.int32) * BLK + reach + block_low

    def take_window(start_row):
        return lax.dynamic_slice_in_dim(padded, start_row, span, 1)

    windows = jax.vmap(take_window, out_axes=1)(starts)
    key_block = windows[0]
    value_block = windows[1]
    key_dot = windows[2]
    value_dot = windows[3]
    query_block = queries.reshape(block_count, BLK, heads_here, HD)
    query_dot = query_tangent.reshape(block_count, BLK, heads_here, HD)
    query_pos = first_pos + jnp.arange(tokens_here, dtype=jnp.int32).reshape(block_count, BLK)
    key_pos = first_pos + starts[:, None] - reach + jnp.arange(span, dtype=jnp.int32)[None, :]
    relative = key_pos[:, None, :] - query_pos[:, :, None]
    window_low = block_low[:, None, None]
    inside = (relative >= window_low) & (relative < window_low + WIN)
    inside = inside & ((key_pos >= 0) & (key_pos < total_tokens))[:, None, :]
    inside = inside[:, None]
    scores = (
        jnp.einsum("bqhd,bkhd->bhqk", query_block, key_block, preferred_element_type=jnp.float32)
        * score_scale
    )
    scores = jnp.where(inside, scores, -1e30)
    peak_val = jnp.max(scores, axis=-1, keepdims=True)
    expo_val = jnp.where(inside, jnp.exp(scores - peak_val), 0.0)
    weights = expo_val / jnp.sum(expo_val, axis=-1, keepdims=True)
    score_dot = jnp.einsum(
        "bqhd,bkhd->bhqk", query_dot, key_block, preferred_element_type=jnp.float32
    )
    score_dot = (
        score_dot
        + jnp.einsum("bqhd,bkhd->bhqk", query_block, key_dot, preferred_element_type=jnp.float32)
    ) * score_scale
    weight_dot = weights * (score_dot - jnp.sum(weights * score_dot, axis=-1, keepdims=True))
    weights_low = weights.astype(jnp.bfloat16)
    weight_dot_low = weight_dot.astype(jnp.bfloat16)
    attended = jnp.einsum(
        "bhqk,bkhd->bqhd", weights_low, value_block, preferred_element_type=jnp.float32
    )
    attended_tangent = jnp.einsum(
        "bhqk,bkhd->bqhd", weight_dot_low, value_block, preferred_element_type=jnp.float32
    )
    attended_tangent = attended_tangent + jnp.einsum(
        "bhqk,bkhd->bqhd", weights_low, value_dot, preferred_element_type=jnp.float32
    )
    attended = attended.astype(jnp.bfloat16).reshape(tokens_here, width_here)
    attended_tangent = attended_tangent.astype(jnp.bfloat16).reshape(tokens_here, width_here)
    branch_term = jnp.dot(
        attended,
        lax.all_gather(out_proj, "seq", axis=1, tiled=True),
        preferred_element_type=jnp.float32,
    )
    tangent_term = jnp.dot(
        attended_tangent,
        lax.all_gather(out_proj, "seq", axis=1, tiled=True),
        preferred_element_type=jnp.float32,
    )
    branch, branch_tangent = (
        lax.psum_scatter(branch_term, "tp", scatter_dimension=1, tiled=True),
        lax.psum_scatter(tangent_term, "tp", scatter_dimension=1, tiled=True),
    )
    student_out = cosine * noisy - sine_t * branch
    student_tangent = (
        -sine_t * noisy + cosine * velocity - cosine * branch - sine_t * branch_tangent
    )
    return (student_out, student_tangent)


def solution(mesh):
    return jax.shard_map(
        body,
        mesh=mesh,
        in_specs=(
            P("seq", "tp"),
            P("seq", "tp"),
            P("seq"),
            P("seq"),
            P("seq", "tp"),
            P("tp", "seq"),
            P("seq", "tp"),
            P("seq", "tp"),
            P("seq", "tp"),
            P("seq", "tp"),
            P("seq", "tp"),
            P("seq", "tp"),
            P("tp", "seq"),
        ),
        out_specs=(P("seq", "tp"), P("seq", "tp")),
        check_vma=False,
    )
```

profile of v0, /device:TPU:1, one launch (start us, length us, event | category | flops | bytes accessed | tf_op | source)
XLA Modules:
  0.0 496.5 jit_solution(10031335165689679332)
XLA Ops:
  15.4 5.6 %collective-permute-start = (bf16[4,192,640]{2,1,0:T(8,128)(2,1)}, bf16[4,192,640]{2,1,0:T(8,128)(2,1)S(1)}, u32[]{:S(2)}, u32[]{:S(2)}) collective-permute-start(bf16[4,192,640]{2,1,0:T(8,128)(2,1)} %copy.36), channel_id=1, source_target_pairs={{0,4},{4,8},{8,12},{12,16},{16,20},{20,24},{24,28},{28,32},{32,36}... | collective-permute-start | bytes 2949128 | tf_op jit(solution)/shard_map/ppermute | solution.py:19
  26.1 37.4 %collective-permute-done = bf16[4,192,640]{2,1,0:T(8,128)(2,1)S(1)} collective-permute-done((bf16[4,192,640]{2,1,0:T(8,128)(2,1)}, bf16[4,192,640]{2,1,0:T(8,128)(2,1)S(1)}, u32[]{:S(2)}, u32[]{:S(2)}) %collective-permute-start) | collective-permute-done | bytes 983072 | tf_op jit(solution)/shard_map/ppermute | solution.py:19
  67.0 5.7 %pad_maximum_fusion = bf16[4,640,640]{1,2,0:T(8,128)(2,1)} fusion(bf16[4,192,640]{1,2,0:T(8,128)(2,1)S(1)} %copy.39, bf16[1,256,640]{1,2,0:T(8,128)(2,1)} %bitcast.93, bf16[1,256,640]{1,2,0:T(8,128)(2,1)} %bitcast.91, bf16[1,256,640]{1,2,0:T(8,128)(2,1)} %bitcast.89, bf16[1,256,640]{1,2,0:T(8,128)(2,1)S(1)} %bitcast.87, bf16[4,192,640]{1,2,0:T(8,128)(2,1)S(1)} %copy.38), kind=kLoop, calls=%fused_computation.4 | loop fusion | flops 19660800 | bytes 6553600 | tf_op jit(solution)/shard_map/concatenate | solution.py:23
  72.7 41.2 %while.1 = (s32[]{:T(128)}, bf16[4,640,5,128]{1,3,2,0:T(8,128)(2,1)}, s32[4,4]{1,0:T(4,128)S(1)}, bf16[4,4,320,5,128]{4,2,3,0,1:T(8,128)(2,1)}, s32[]{:T(128)}) while((s32[]{:T(128)}, bf16[4,640,5,128]{1,3,2,0:T(8,128)(2,1)}, s32[4,4]{1,0:T(4,128)S(1)}, bf16[4,4,320,5,128]{4,2,3,0,1:T(8,128)(2,1)}, s32[]{:T(128)}) %tuple.43), condition=%wide.while_cond, body=%wide.while_body.sunk | while | flops 2 | bytes 9831021 | solution.py:69
  73.3 4.7 constant_dynamic-slice_fusion.5
  78.0 3.5 copy.77
  83.6 4.7 constant_dynamic-slice_fusion.5
  88.3 3.5 copy.77
  93.9 4.7 constant_dynamic-slice_fusion.5
  98.6 3.5 copy.77
  104.2 4.5 constant_dynamic-slice_fusion.5
  108.8 3.5 copy.77
  113.9 3.8 fusion.40
  117.6 2.6 fusion.14
  120.5 46.9 %all-gather.3.cloned.1.call-done = bf16[640,5120]{0,1:T(8,128)(2,1)} async-done(((bf16[640,80]{0,1:T(8,128)(2,1)}), bf16[640,5120]{0,1:T(8,128)(2,1)}) %all-gather.3.cloned.1.call-update) | async-done | bytes 6553616 | tf_op jit(solution)/shard_map/all_gather | solution.py:116
  167.3 7.4 %fusion.28 = f32[256,5120]{1,0:T(8,128)} fusion(bf16[640,5120]{0,1:T(8,128)(2,1)} %all-gather.3.cloned.1.call-done, bf16[32,8,5,128]{3,2,1,0:T(8,128)(2,1)S(1)} %bitcast.94), kind=kOutput, calls=%fused_computation.47 | convolution fusion | flops 1677721600 | bytes 12124160 | tf_op jit(solution)/shard_map/dot_general | solution.py:114
  178.4 2.7 fusion.5
  185.0 4.6 fusion.25
  189.7 116.9 %all-gather.5.cloned.1.call-done = bf16[640,5120]{0,1:T(8,128)(2,1)} async-done(((bf16[640,80]{0,1:T(8,128)(2,1)}), bf16[640,5120]{0,1:T(8,128)(2,1)}) %all-gather.5.cloned.1.call-update) | async-done | bytes 6553616 | tf_op jit(solution)/shard_map/all_gather | solution.py:54
  306.5 7.3 %fusion.45 = f32[256,5120]{1,0:T(8,128)} fusion(bf16[256,640]{1,0:T(8,128)(2,1)S(1)} %copy-done, bf16[640,5120]{0,1:T(8,128)(2,1)} %all-gather.5.cloned.1.call-done), kind=kOutput, calls=%fused_computation.70 | convolution fusion | flops 1677721600 | bytes 12124160 | tf_op jit(solution)/shard_map/dot_general | solution.py:52
  314.9 51.1 %reduce-scatter.4.cloned.1.call-done = f32[256,1280]{1,0:T(8,128)} async-done(((f32[256,5120]{1,0:T(8,128)}), f32[256,1280]{1,0:T(8,128)}) %reduce-scatter.4.cloned.1.call-update) | async-done | bytes 1310736 | tf_op jit(solution)/shard_map/reduce_scatter | solution.py:125
  366.0 59.8 %reduce-scatter.8.cloned.1.call-done = f32[256,1280]{1,0:T(8,128)} async-done(((f32[256,5120]{1,0:T(8,128)}), f32[256,1280]{1,0:T(8,128)}) %reduce-scatter.8.cloned.1.call-update) | async-done | bytes 1310736 | tf_op jit(solution)/shard_map/reduce_scatter | solution.py:126
  425.9 59.8 %reduce-scatter.6.cloned.1.call-done = f32[256,1280]{1,0:T(8,128)} async-done(((f32[256,5120]{1,0:T(8,128)}), f32[256,1280]{1,0:T(8,128)}) %reduce-scatter.6.cloned.1.call-update) | async-done | bytes 1310736 | tf_op jit(solution)/shard_map/reduce_scatter | solution.py:57
  485.7 4.3 multiply_subtract_fusion
  (94 shorter events, 34.1 us)
Async XLA Ops:
  7.2 299.4 %copy-start = (bf16[256,640]{1,0:T(8,128)(2,1)S(1)}, bf16[256,640]{1,0:T(8,128)(2,1)}, u32[]{:S(2)}) copy-start(bf16[256,640]{1,0:T(8,128)(2,1)} %param.17) | copy-start | bytes 983044
  7.2 5.1 %copy-start.7 = (bf16[256,640]{1,0:T(8,128)(2,1)S(1)}, bf16[256,640]{1,0:T(8,128)(2,1)}, u32[]{:S(2)}) copy-start(bf16[256,640]{1,0:T(8,128)(2,1)} %param.24) | copy-start | bytes 983044
  7.2 160.1 %all-gather.3.cloned.1.call-start = ((), (), s32[]{:S(2)}) async-start(), calls=%async_computation.3 | async-start | bytes 6656000 | tf_op jit(solution)/shard_map/all_gather | solution.py:116
  7.9 298.6 %all-gather.5.cloned.1.call-start = ((), (), s32[]{:S(2)}) async-start(), calls=%async_computation.5 | async-start | bytes 6656000 | tf_op jit(solution)/shard_map/all_gather | solution.py:54
  8.7 357.4 %reduce-scatter.4.cloned.1.call-start = ((), (), s32[]{:S(2)}) async-start(), calls=%async_computation.4 | async-start | bytes 6553600 | tf_op jit(solution)/shard_map/reduce_scatter | solution.py:125
  11.0 1.5 copy-start.1
  12.3 0.7 copy-start.2
  12.5 0.7 copy-start.3
  14.0 9.8 %copy-start.10 = (s32[4]{0:T(128)S(1)}, s32[4]{0:T(128)}, u32[]{:S(2)}) copy-start(s32[4]{0:T(128)} %param.16) | copy-start | bytes 52
  15.4 8.5 %copy-start.8 = (bf16[256,640]{1,0:T(8,128)(2,1)S(1)}, bf16[256,640]{1,0:T(8,128)(2,1)}, u32[]{:S(2)}) copy-start(bf16[256,640]{1,0:T(8,128)(2,1)} %param.19) | copy-start | bytes 983044
  15.4 48.1 %collective-permute-start = (bf16[4,192,640]{2,1,0:T(8,128)(2,1)}, bf16[4,192,640]{2,1,0:T(8,128)(2,1)S(1)}, u32[]{:S(2)}, u32[]{:S(2)}) collective-permute-start(bf16[4,192,640]{2,1,0:T(8,128)(2,1)} %copy.36), channel_id=1, source_target_pairs={{0,4},{4,8},{8,12},{12,16},{16,20},{20,24},{24,28},{28,32},{32,36}... | collective-permute-start | bytes 2949128 | tf_op jit(solution)/shard_map/ppermute | solution.py:19
  22.4 43.1 %collective-permute-start.1 = (bf16[4,192,640]{2,1,0:T(8,128)(2,1)}, bf16[4,192,640]{2,1,0:T(8,128)(2,1)}, u32[]{:S(2)}, u32[]{:S(2)}) collective-permute-start(bf16[4,192,640]{2,1,0:T(8,128)(2,1)} %copy.37), channel_id=1, source_target_pairs={{4,0},{8,4},{12,8},{16,12},{20,16},{24,20},{28,24},{32,28},{36,32}... | collective-permute-start | bytes 2949128 | tf_op jit(solution)/shard_map/ppermute | solution.py:22
  72.7 41.2 %copy-start.6 = (bf16[4,64,5,128]{3,2,1,0:T(8,128)(2,1)S(1)}, bf16[4,64,5,128]{3,2,1,0:T(8,128)(2,1)}, u32[]{:S(2)}) copy-start(bf16[4,64,5,128]{3,2,1,0:T(8,128)(2,1)} %reshape.106) | copy-start | bytes 983044
  174.7 1.0 copy-start.9
  174.7 251.1 %reduce-scatter.8.cloned.1.call-start = ((), (), s32[]{:S(2)}) async-start(), calls=%async_computation.7 | async-start | bytes 6553600 | tf_op jit(solution)/shard_map/reduce_scatter | solution.py:126
  176.1 5.0 %slice-start.2 = ((s8[6553600]{0:T(1024)(128)(4,1)}), s8[4194304]{0:T(1024)(128)(4,1)S(1)}, s32[]{:S(2)}) async-start(s8[6553600]{0:T(1024)(128)(4,1)} %bitcast.100), calls=%async_computation.10 | async-start | bytes 8388608
  178.3 3.4 slice-start.3
  178.3 3.4 copy-start.12
  181.8 2.2 slice-start
  182.8 2.2 slice-start.1
  189.6 296.1 %reduce-scatter.6.cloned.1.call-start = ((), (), s32[]{:S(2)}) async-start(), calls=%async_computation.6 | async-start | bytes 6553600 | tf_op jit(solution)/shard_map/reduce_scatter | solution.py:57
  313.9 0.7 copy-start.11
  313.9 171.8 %copy-start.4 = (bf16[256,1280]{1,0:T(8,128)(2,1)S(1)}, bf16[256,1280]{1,0:T(8,128)(2,1)}, u32[]{:S(2)}) copy-start(bf16[256,1280]{1,0:T(8,128)(2,1)} %param.14) | copy-start | bytes 1966084
  313.9 171.8 %copy-start.5 = (bf16[256,1280]{1,0:T(8,128)(2,1)S(1)}, bf16[256,1280]{1,0:T(8,128)(2,1)}, u32[]{:S(2)}) copy-start(bf16[256,1280]{1,0:T(8,128)(2,1)} %param.13) | copy-start | bytes 1966084
Sparse Core Ops, SparseCore 0:
  11.5 155.8 all-gather.2
  170.8 135.6 all-gather.4
  309.1 56.9 reduce-scatter.3
  368.5 57.3 reduce-scatter.7
  428.3 57.3 reduce-scatter.5
where the time goes:
time: 497 us
  waiting for transfers between devices  375 us (75%)
  local copies, waits for them, and re-layouts  57 us (11%)
  matrix products  32.1 us (6%)
  between operations  14 us (3%)
  other arithmetic  11.3 us (2%)
  starting transfers between devices  7.3 us (1%)
    all_gather x1, waiting for transfers between devices, body(): lax.all_gather(teacher_proj, 'seq', axis=1, tiled=True)  117 us
    reduce_scatter x1, waiting for transfers between devices, body(): lax.psum_scatter(tangent_term, 'tp', scatter_dimension=1, tiled=True)  59.8 us
    reduce_scatter x1, waiting for transfers between devices, body(): lax.psum_scatter(teacher_term, 'tp', scatter_dimension=1, tiled=True)  59.8 us
    reduce_scatter x1, waiting for transfers between devices, body(): lax.psum_scatter(branch_term, 'tp', scatter_dimension=1, tiled=True)  51.1 us
    all_gather x1, waiting for transfers between devices, body(): lax.all_gather(out_proj, 'seq', axis=1, tiled=True)  46.9 us
    gather x20, local copies, waits for them, and re-layouts  41.1 us
    ppermute x1, waiting for transfers between devices, padded_2(): lax.ppermute(lax.slice_in_dim(block, block.shape[dim] - width, None, axis...  37.4 us
  transfers between devices with their start and end apart: 7, of which 7 were waited for; matrix products, arithmetic and copies ran while one was open for 19% of the time, Pallas kernels for 0%

commit v1 on v0

--- a/solution.py
+++ b/solution.py
@@ -51,7 +51,9 @@
     noisy = cosine * latents.astype(jnp.float32) + sine_t * noise.astype(jnp.float32)
     teacher_term = jnp.dot(
         teacher_heads,
-        lax.all_gather(teacher_proj, "seq", axis=1, tiled=True),
+        jnp.concatenate(
+            lax.all_to_all(jnp.stack([teacher_proj] * lax.axis_size("seq")), "seq", 0, 0), axis=1
+        ),
         preferred_element_type=jnp.float32,
     )
     velocity = lax.psum_scatter(teacher_term, "tp", scatter_dimension=1, tiled=True)

time: 497 us -> 433 us (0.87)
  waiting for transfers between devices: 375 us -> 299 us
  starting transfers between devices: 7.3 us -> 15.3 us
    all_to_all x0 -> x1, waiting for transfers between devices: none -> 128 us  [body(): lax.all_to_all(jnp.stack([teacher_proj] * lax.axis_size('seq')), 'seq', 0...]
    all_gather x1 -> x0, waiting for transfers between devices: 117 us -> none  [body(): lax.all_gather(teacher_proj, 'seq', axis=1, tiled=True)]
    reduce_scatter x1, waiting for transfers between devices: 51.1 us -> 0.01 us  [body(): lax.psum_scatter(branch_term, 'tp', scatter_dimension=1, tiled=True)]
    reduce_scatter x1, waiting for transfers between devices: 59.8 us -> 18.6 us  [body(): lax.psum_scatter(tangent_term, 'tp', scatter_dimension=1, tiled=True)]
    all_to_all x0 -> x1, starting transfers between devices: none -> 8.23 us  [body(): lax.all_to_all(jnp.stack([teacher_proj] * lax.axis_size('seq')), 'seq', 0...]
    all_gather x1, waiting for transfers between devices: 46.9 us -> 52.3 us  [body(): lax.all_gather(out_proj, 'seq', axis=1, tiled=True)]
  transfers between devices with their start and end apart: 7 -> 7, of which waited for: 7 -> 6; matrix products, arithmetic and copies ran while one was open for 19% -> 20% of each run, Pallas kernels for 0% -> 0%
where the time goes in v1:
time: 433 us; the launch traced here: 432 us
  waiting for transfers between devices  299 us (69%)
  local copies, waits for them, and re-layouts  60.4 us (14%)
  matrix products  32.3 us (7%)
  starting transfers between devices  15.3 us (4%)
  between operations  14 us (3%)
  other arithmetic  11.4 us (3%)
    all_to_all x1, waiting for transfers between devices, body(): lax.all_to_all(jnp.stack([teacher_proj] * lax.axis_size('seq')), 'seq', 0...  128 us
    reduce_scatter x1, waiting for transfers between devices, body(): lax.psum_scatter(teacher_term, 'tp', scatter_dimension=1, tiled=True)  60.5 us
    all_gather x1, waiting for transfers between devices, body(): lax.all_gather(out_proj, 'seq', axis=1, tiled=True)  52.3 us
    gather x20, local copies, waits for them, and re-layouts  41.1 us
    ppermute x1, waiting for transfers between devices, padded_2(): lax.ppermute(lax.slice_in_dim(block, block.shape[dim] - width, None, axis...  37.4 us
    reduce_scatter x1, waiting for transfers between devices, body(): lax.psum_scatter(tangent_term, 'tp', scatter_dimension=1, tiled=True)  18.6 us
  transfers between devices with their start and end apart: 7, of which 6 were waited for; matrix products, arithmetic and copies ran while one was open for 20% of the time, Pallas kernels for 0%

profile of v1, /device:TPU:1, one launch (start us, length us, event | category | flops | bytes accessed | tf_op | source)
XLA Modules:
  0.0 432.1 jit_solution(16459258443561854225)
XLA Ops:
  14.6 5.6 %collective-permute-start = (bf16[4,192,640]{2,1,0:T(8,128)(2,1)}, bf16[4,192,640]{2,1,0:T(8,128)(2,1)S(1)}, u32[]{:S(2)}, u32[]{:S(2)}) collective-permute-start(bf16[4,192,640]{2,1,0:T(8,128)(2,1)} %copy.37), channel_id=1, source_target_pairs={{0,4},{4,8},{8,12},{12,16},{16,20},{20,24},{24,28},{28,32},{32,36}... | collective-permute-start | bytes 2949128 | tf_op jit(solution)/shard_map/ppermute | solution.py:19
  25.3 37.4 %collective-permute-done = bf16[4,192,640]{2,1,0:T(8,128)(2,1)S(1)} collective-permute-done((bf16[4,192,640]{2,1,0:T(8,128)(2,1)}, bf16[4,192,640]{2,1,0:T(8,128)(2,1)S(1)}, u32[]{:S(2)}, u32[]{:S(2)}) %collective-permute-start) | collective-permute-done | bytes 983072 | tf_op jit(solution)/shard_map/ppermute | solution.py:19
  66.3 5.7 %pad_maximum_fusion = bf16[4,640,640]{1,2,0:T(8,128)(2,1)} fusion(bf16[4,192,640]{1,2,0:T(8,128)(2,1)S(1)} %copy.40, bf16[1,256,640]{1,2,0:T(8,128)(2,1)} %bitcast.96, bf16[1,256,640]{1,2,0:T(8,128)(2,1)} %bitcast.94, bf16[1,256,640]{1,2,0:T(8,128)(2,1)} %bitcast.92, bf16[1,256,640]{1,2,0:T(8,128)(2,1)S(1)} %bitcast.90, bf16[4,192,640]{1,2,0:T(8,128)(2,1)S(1)} %copy.39), kind=kLoop, calls=%fused_computation.4 | loop fusion | flops 19660800 | bytes 6553600 | tf_op jit(solution)/shard_map/concatenate | solution.py:23
  72.0 41.2 %while.1 = (s32[]{:T(128)}, bf16[4,640,5,128]{1,3,2,0:T(8,128)(2,1)}, s32[4,4]{1,0:T(4,128)S(1)}, bf16[4,4,320,5,128]{4,2,3,0,1:T(8,128)(2,1)}, s32[]{:T(128)}) while((s32[]{:T(128)}, bf16[4,640,5,128]{1,3,2,0:T(8,128)(2,1)}, s32[4,4]{1,0:T(4,128)S(1)}, bf16[4,4,320,5,128]{4,2,3,0,1:T(8,128)(2,1)}, s32[]{:T(128)}) %tuple.41), condition=%wide.while_cond, body=%wide.while_body.sunk | while | flops 2 | bytes 9831021 | solution.py:71
  72.6 4.7 %constant_dynamic-slice_fusion.5 = bf16[4,320,5,128]{1,3,2,0:T(8,128)(2,1)} fusion(bf16[4,640,5,128]{1,3,2,0:T(8,128)(2,1)} %get-tuple-element.76, s32[]{:T(128)} %bitcast.83), kind=kLoop, calls=%fused_computation.2.clone.1 | loop fusion | bytes 3276804 | tf_op jit(solution)/shard_map/vmap()/gather
  77.3 3.5 copy.78
  82.9 4.7 %constant_dynamic-slice_fusion.5 = bf16[4,320,5,128]{1,3,2,0:T(8,128)(2,1)} fusion(bf16[4,640,5,128]{1,3,2,0:T(8,128)(2,1)} %get-tuple-element.76, s32[]{:T(128)} %bitcast.83), kind=kLoop, calls=%fused_computation.2.clone.1 | loop fusion | bytes 3276804 | tf_op jit(solution)/shard_map/vmap()/gather
  87.6 3.5 copy.78
  93.2 4.7 %constant_dynamic-slice_fusion.5 = bf16[4,320,5,128]{1,3,2,0:T(8,128)(2,1)} fusion(bf16[4,640,5,128]{1,3,2,0:T(8,128)(2,1)} %get-tuple-element.76, s32[]{:T(128)} %bitcast.83), kind=kLoop, calls=%fused_computation.2.clone.1 | loop fusion | bytes 3276804 | tf_op jit(solution)/shard_map/vmap()/gather
  97.9 3.5 copy.78
  103.6 4.5 %constant_dynamic-slice_fusion.5 = bf16[4,320,5,128]{1,3,2,0:T(8,128)(2,1)} fusion(bf16[4,640,5,128]{1,3,2,0:T(8,128)(2,1)} %get-tuple-element.76, s32[]{:T(128)} %bitcast.83), kind=kLoop, calls=%fused_computation.2.clone.1 | loop fusion | bytes 3276804 | tf_op jit(solution)/shard_map/vmap()/gather
  108.1 3.5 copy.78
  113.2 3.7 fusion.40
  119.7 52.3 %all-gather.2.cloned.1.call-done = bf16[640,5120]{0,1:T(8,128)(2,1)} async-done(((bf16[640,80]{0,1:T(8,128)(2,1)}), bf16[640,5120]{0,1:T(8,128)(2,1)}) %all-gather.2.cloned.1.call-update) | async-done | bytes 6553616 | tf_op jit(solution)/shard_map/all_gather | solution.py:118
  172.0 7.5 %fusion.28 = f32[256,5120]{1,0:T(8,128)} fusion(bf16[640,5120]{0,1:T(8,128)(2,1)} %all-gather.2.cloned.1.call-done, bf16[32,8,5,128]{3,2,1,0:T(8,128)(2,1)S(1)} %bitcast.97), kind=kOutput, calls=%fused_computation.47 | convolution fusion | flops 1677721600 | bytes 12124160 | tf_op jit(solution)/shard_map/dot_general | solution.py:116
  180.4 3.3 stack.17
  183.7 8.2 %all-to-all-start = ((bf16[64,640,80]{1,2,0:T(8,128)(2,1)}), bf16[64,640,80]{1,2,0:T(8,128)(2,1)}, u32[]{:S(2)}, u32[]{:S(2)}) async-start(bf16[64,640,80]{1,2,0:T(8,128)(2,1)} %stack.17), calls=%async_computation.1 | async-start | bytes 13107200 | tf_op jit(solution)/shard_map/all_to_all | solution.py:55
  194.7 2.7 fusion.5
  201.3 4.6 %fusion.25 = f32[256,5120]{1,0:T(8,128)} fusion(bf16[640,5120]{0,1:T(8,128)(2,1)S(1)} %bitcast.88, bf16[32,8,5,128]{3,2,1,0:T(8,128)(2,1)S(1)} %bitcast.98), kind=kOutput, calls=%fused_computation.44 | convolution fusion | flops 1677721600 | bytes 12124160 | tf_op jit(solution)/shard_map/dot_general | solution.py:121
  205.9 127.8 %all-to-all-done = bf16[64,640,80]{1,2,0:T(8,128)(2,1)} async-done(((bf16[64,640,80]{1,2,0:T(8,128)(2,1)}), bf16[64,640,80]{1,2,0:T(8,128)(2,1)}, u32[]{:S(2)}, u32[]{:S(2)}) %all-to-all-start) | async-done | bytes 6553632 | tf_op jit(solution)/shard_map/all_to_all | solution.py:55
  333.7 7.4 %fusion.45 = f32[256,5120]{1,0:T(8,128)} fusion(bf16[256,640]{1,0:T(8,128)(2,1)S(1)} %copy-done, bf16[640,5120]{0,1:T(8,128)(2,1)} %bitcast.12), kind=kOutput, calls=%fused_computation.70 | convolution fusion | flops 1677721600 | bytes 12124160 | tf_op jit(solution)/shard_map/dot_general | solution.py:52
  342.1 18.6 %reduce-scatter.8.cloned.1.call-done = f32[256,1280]{1,0:T(8,128)} async-done(((f32[256,5120]{1,0:T(8,128)}), f32[256,1280]{1,0:T(8,128)}) %reduce-scatter.8.cloned.1.call-update) | async-done | bytes 1310736 | tf_op jit(solution)/shard_map/reduce_scatter | solution.py:128
  360.7 60.5 %reduce-scatter.6.cloned.1.call-done = f32[256,1280]{1,0:T(8,128)} async-done(((f32[256,5120]{1,0:T(8,128)}), f32[256,1280]{1,0:T(8,128)}) %reduce-scatter.6.cloned.1.call-update) | async-done | bytes 1310736 | tf_op jit(solution)/shard_map/reduce_scatter | solution.py:59
  421.2 4.3 %multiply_subtract_fusion = (f32[256,1280]{1,0:T(8,128)}, f32[256,1280]{1,0:T(8,128)}) fusion(f32[256,1280]{1,0:T(8,128)} %reduce-scatter.8.cloned.1.call-done, f32[256,1280]{1,0:T(8,128)} %reduce-scatter.4.cloned.1.call-done, f32[256,1280]{1,0:T(8,128)} %reduce-scatter.6.cloned.1.call-done, bf16[256,1280]{1,0:T(8,128)(2,1)S(1)} %copy-done.4, ...), kind=kLoop, calls=%fused_computation.25 | loop fusion | flops 4915200 | bytes 7867392 | tf_op jit(solution)/shard_map/sub | solution.py:132
  (96 shorter events, 35.9 us)
Async XLA Ops:
  7.2 326.6 %copy-start = (bf16[256,640]{1,0:T(8,128)(2,1)S(1)}, bf16[256,640]{1,0:T(8,128)(2,1)}, u32[]{:S(2)}) copy-start(bf16[256,640]{1,0:T(8,128)(2,1)} %param.17) | copy-start | bytes 983044
  7.2 4.4 %copy-start.7 = (bf16[256,640]{1,0:T(8,128)(2,1)S(1)}, bf16[256,640]{1,0:T(8,128)(2,1)}, u32[]{:S(2)}) copy-start(bf16[256,640]{1,0:T(8,128)(2,1)} %param.24) | copy-start | bytes 983044
  7.2 164.8 %all-gather.2.cloned.1.call-start = ((), (), s32[]{:S(2)}) async-start(), calls=%async_computation.4 | async-start | bytes 6656000 | tf_op jit(solution)/shard_map/all_gather | solution.py:118
  7.9 334.2 %reduce-scatter.4.cloned.1.call-start = ((), (), s32[]{:S(2)}) async-start(), calls=%async_computation.5 | async-start | bytes 6553600 | tf_op jit(solution)/shard_map/reduce_scatter | solution.py:127
  10.3 1.5 copy-start.1
  11.5 0.7 copy-start.2
  11.7 0.7 copy-start.3
  13.2 9.8 %copy-start.11 = (s32[4]{0:T(128)S(1)}, s32[4]{0:T(128)}, u32[]{:S(2)}) copy-start(s32[4]{0:T(128)} %param.16) | copy-start | bytes 52
  14.6 8.5 %copy-start.8 = (bf16[256,640]{1,0:T(8,128)(2,1)S(1)}, bf16[256,640]{1,0:T(8,128)(2,1)}, u32[]{:S(2)}) copy-start(bf16[256,640]{1,0:T(8,128)(2,1)} %param.19) | copy-start | bytes 983044
  14.6 48.1 %collective-permute-start = (bf16[4,192,640]{2,1,0:T(8,128)(2,1)}, bf16[4,192,640]{2,1,0:T(8,128)(2,1)S(1)}, u32[]{:S(2)}, u32[]{:S(2)}) collective-permute-start(bf16[4,192,640]{2,1,0:T(8,128)(2,1)} %copy.37), channel_id=1, source_target_pairs={{0,4},{4,8},{8,12},{12,16},{16,20},{20,24},{24,28},{28,32},{32,36}... | collective-permute-start | bytes 2949128 | tf_op jit(solution)/shard_map/ppermute | solution.py:19
  21.6 43.1 %collective-permute-start.1 = (bf16[4,192,640]{2,1,0:T(8,128)(2,1)}, bf16[4,192,640]{2,1,0:T(8,128)(2,1)}, u32[]{:S(2)}, u32[]{:S(2)}) collective-permute-start(bf16[4,192,640]{2,1,0:T(8,128)(2,1)} %copy.38), channel_id=1, source_target_pairs={{4,0},{8,4},{12,8},{16,12},{20,16},{24,20},{28,24},{32,28},{36,32}... | collective-permute-start | bytes 2949128 | tf_op jit(solution)/shard_map/ppermute | solution.py:22
  72.0 41.2 %copy-start.6 = (bf16[4,64,5,128]{3,2,1,0:T(8,128)(2,1)S(1)}, bf16[4,64,5,128]{3,2,1,0:T(8,128)(2,1)}, u32[]{:S(2)}) copy-start(bf16[4,64,5,128]{3,2,1,0:T(8,128)(2,1)} %reshape.114) | copy-start | bytes 983044
  179.5 0.9 copy-start.10
  183.7 8.3 %copy-start.9 = (bf16[256,640]{1,0:T(8,128)(2,1)S(1)}, bf16[256,640]{1,0:T(8,128)(2,1)}, u32[]{:S(2)}) copy-start(bf16[256,640]{1,0:T(8,128)(2,1)} %param.22) | copy-start | bytes 983044
  183.7 150.1 %all-to-all-start = ((bf16[64,640,80]{1,2,0:T(8,128)(2,1)}), bf16[64,640,80]{1,2,0:T(8,128)(2,1)}, u32[]{:S(2)}, u32[]{:S(2)}) async-start(bf16[64,640,80]{1,2,0:T(8,128)(2,1)} %stack.17), calls=%async_computation.1 | async-start | bytes 13107200 | tf_op jit(solution)/shard_map/all_to_all | solution.py:55
  191.9 168.8 %reduce-scatter.8.cloned.1.call-start = ((), (), s32[]{:S(2)}) async-start(), calls=%async_computation.7 | async-start | bytes 6553600 | tf_op jit(solution)/shard_map/reduce_scatter | solution.py:128
  192.3 5.1 %slice-start.2 = ((s8[6553600]{0:T(1024)(128)(4,1)}), s8[4194304]{0:T(1024)(128)(4,1)S(1)}, s32[]{:S(2)}) async-start(s8[6553600]{0:T(1024)(128)(4,1)} %bitcast.103), calls=%async_computation.10 | async-start | bytes 8388608
  194.6 3.4 slice-start.3
  194.6 3.4 copy-start.13
  198.1 2.2 slice-start
  199.1 2.2 slice-start.1
  205.9 215.3 %reduce-scatter.6.cloned.1.call-start = ((), (), s32[]{:S(2)}) async-start(), calls=%async_computation.6 | async-start | bytes 6553600 | tf_op jit(solution)/shard_map/reduce_scatter | solution.py:59
  341.1 80.1 %copy-start.4 = (bf16[256,1280]{1,0:T(8,128)(2,1)S(1)}, bf16[256,1280]{1,0:T(8,128)(2,1)}, u32[]{:S(2)}) copy-start(bf16[256,1280]{1,0:T(8,128)(2,1)} %param.14) | copy-start | bytes 1966084
  341.1 80.1 %copy-start.5 = (bf16[256,1280]{1,0:T(8,128)(2,1)S(1)}, bf16[256,1280]{1,0:T(8,128)(2,1)}, u32[]{:S(2)}) copy-start(bf16[256,1280]{1,0:T(8,128)(2,1)} %param.13) | copy-start | bytes 1966084
  (1 other events, 0.7 us)
Sparse Core Ops, SparseCore 0:
  11.5 160.4 all-gather.1
  179.6 106.2 reduce-scatter.3
  288.4 72.2 reduce-scatter.7
  363.2 58.0 reduce-scatter.5
